TPU v7x, 512 devices: a whole 4x8x8 slice. The times are simulated.
512 devices in a mesh: row: 64 (over x, z, core), col: 8 (over y).
Axes of the slice: x: 4, y: 8, z: 8, core: 2. Of those that a mesh axis runs over, the one named last changes fastest.
Arguments:
- trailing: float32 [32768, 8192], P('row', 'col'), may hold values from -6 to 6
- reflectors: float32 [32768, 256], P('row', 'col'), may hold values from -0.25 to 0.25
- leaf_factor: float32 [16384, 256], P('row', 'col'), may hold values from -0.5 to 0.5
- node_reflect: float32 [6, 16384, 256], P(None, 'row', 'col'), may hold values from -0.375 to 0.375
- node_factor: float32 [6, 16384, 256], P(None, 'row', 'col'), may hold values from -0.5 to 0.5
Outputs:
- updated: float32 [32768, 8192], P('row', 'col')
All inputs are finite; a program needn't handle non-finite values.
Results may differ from a plain program's by a relative error of at most 0.00014.
Values sent between devices are 32-bit elements; how exact they have to be, the bound alone decides.
A program may use at most 64 MiB of HBM per device.

v0:
```python
import jax
import jax.numpy as jnp
from jax import lax
from jax.sharding import PartitionSpec as P

B = 256


highest = lax.Precision.HIGHEST


def turned_gather(arrays, axis, dims):
    turned = [jnp.moveaxis(a, dim, 0) for a, dim in zip(arrays, dims)]
    both = jnp.concatenate([t.reshape(len(t), -1) for t in turned], axis=1)
    whole, at, done = (lax.all_gather(both, axis, axis=0, tiled=True), 0, [])
    for t, dim in zip(turned, dims):
        section = whole[:, at : at + t[0].size].reshape(-1, *t.shape[1:])
        done.append(jnp.moveaxis(section, 0, dim))
        at += t[0].size
    return tuple(done)


def swapped(value, axis, apart):
    mask = 2**apart
    pairs = [(source, source ^ mask) for source in range(lax.axis_size(axis))]
    return lax.ppermute(value, axis, pairs)


def triangle(factor):
    return jnp.triu(factor) + 0.5 * jnp.eye(factor.shape[-1], dtype=factor.dtype)


def combine(upper_rows, partner_rows, other_piece, node_y, node_full, clear):
    chosen_y = jnp.where(clear, other_piece, node_y)
    chosen_tri = triangle(jnp.where(clear, node_full, other_piece))
    leader_rows = jnp.where(clear, upper_rows, partner_rows)
    follower_rows = jnp.where(clear, partner_rows, upper_rows)
    summed = leader_rows + jnp.einsum("kb,kc->bc", chosen_y, follower_rows, precision=highest)
    coupling = jnp.einsum("kb,kc->bc", chosen_tri, summed, precision=highest)
    lowered = upper_rows - jnp.einsum("bk,kc->bc", chosen_y, coupling, precision=highest)
    return jnp.where(clear, upper_rows - coupling, lowered)


def per_device(trailing, reflectors, leaf_factor, node_reflect, node_factor):
    vectors, leaf_full, node_y_all, node_f_all = turned_gather(
        (reflectors, leaf_factor, node_reflect, node_factor), "col", (1, 1, 2, 2)
    )
    leaf_tri = triangle(leaf_full)
    inner = jnp.einsum("rb,rc->bc", vectors, trailing, precision=highest)
    scaled = jnp.einsum("kb,kc->bc", leaf_tri, inner, precision=highest)
    leafed = trailing - jnp.einsum("rb,bc->rc", vectors, scaled, precision=highest)
    upper_rows = leafed[:B]
    remainder = leafed[B:]
    position = lax.axis_index("row")
    levels = lax.axis_size("row").bit_length() - 1
    clears = []
    pieces = []
    for section in range(levels):
        clear = position // (1 << section) % 2 == 0
        clears.append(clear)
        pieces.append(jnp.where(clear, node_f_all[section], node_y_all[section]))
    for section in range(levels):
        partner_rows, other_piece = swapped((upper_rows, pieces[section]), "row", section)
        upper_rows = combine(
            upper_rows,
            partner_rows,
            other_piece,
            node_y_all[section],
            node_f_all[section],
            clears[section],
        )
    return jnp.concatenate([upper_rows, remainder], axis=0)


def solution(mesh):
    in_specs = (
        P("row", "col"),
        P("row", "col"),
        P("row", "col"),
        P(None, "row", "col"),
        P(None, "row", "col"),
    )
    out_specs = P("row", "col")
    return jax.shard_map(
        per_device, mesh=mesh, in_specs=in_specs, out_specs=out_specs, check_vma=False
    )
```

profile of v0, /device:TPU:1, one launch (start us, length us, event | category | flops | bytes accessed | tf_op | source)
XLA Modules:
  0.0 352.4 jit_solution(16999531259912984661)
XLA Ops:
  8.6 1.7 pad_maximum_fusion.1
  10.4 59.9 %all-gather.2.cloned.1.call-done = f32[256,3840]{1,0:T(8,128)} async-done(((f32[32,3840]{1,0:T(8,128)}), f32[256,3840]{1,0:T(8,128)}) %all-gather.2.cloned.1.call-update) | async-done | bytes 3932176 | tf_op jit(solution)/shard_map/all_gather | solution.py:15
  70.4 3.1 fusion.43
  73.5 2.1 fusion.45
  75.6 1.9 convolution_subtract_fusion
  78.8 2.7 collective-permute-start.1
  81.5 2.1 fusion.139
  83.6 3.0 copy.12
  86.7 3.0 copy.13
  89.7 3.0 copy.10
  92.7 3.0 copy.11
  95.8 2.1 fusion.70
  97.9 2.1 collective-permute-start
  100.0 1.5 collective-permute-done
  102.6 2.4 fusion.25
  106.1 3.3 collective-permute-start.3
  109.4 2.2 collective-permute-start.2
  111.6 26.6 %collective-permute-done.2 = f32[256,256]{0,1:T(8,128)S(1)} collective-permute-done((f32[256,256]{0,1:T(8,128)S(1)}, f32[256,256]{0,1:T(8,128)S(1)}, u32[]{:S(2)}, u32[]{:S(2)}) %collective-permute-start.2) | collective-permute-done | bytes 262176 | tf_op jit(solution)/shard_map/ppermute | solution.py:26
  141.7 4.4 %collective-permute-start.5 = (f32[256,1024]{1,0:T(8,128)S(1)}, f32[256,1024]{1,0:T(8,128)S(1)}, u32[]{:S(2)}, u32[]{:S(2)}) collective-permute-start(f32[256,1024]{1,0:T(8,128)S(1)} %subtract_select_fusion.4), channel_id=1, source_target_pairs={{0,32},{8,40},{16,48},{24,56},{32,0},{40,8},{48,16},{56,24},{64,96... | collective-permute-start | bytes 3145736 | tf_op jit(solution)/shard_map/ppermute | solution.py:26
  146.0 1.9 collective-permute-start.4
  148.0 54.3 %collective-permute-done.4 = f32[256,256]{0,1:T(8,128)S(1)} collective-permute-done((f32[256,256]{0,1:T(8,128)S(1)}, f32[256,256]{0,1:T(8,128)S(1)}, u32[]{:S(2)}, u32[]{:S(2)}) %collective-permute-start.4) | collective-permute-done | bytes 262176 | tf_op jit(solution)/shard_map/ppermute | solution.py:26
  205.7 8.5 %collective-permute-start.7 = (f32[256,1024]{1,0:T(8,128)S(1)}, f32[256,1024]{1,0:T(8,128)S(1)}, u32[]{:S(2)}, u32[]{:S(2)}) collective-permute-start(f32[256,1024]{1,0:T(8,128)S(1)} %subtract_select_fusion.3), channel_id=1, source_target_pairs={{0,64},{8,72},{16,80},{24,88},{32,96},{40,104},{48,112},{56,120},{... | collective-permute-start | bytes 3145736 | tf_op jit(solution)/shard_map/ppermute | solution.py:26
  214.3 1.9 collective-permute-start.6
  216.2 55.0 %collective-permute-done.6 = f32[256,256]{0,1:T(8,128)S(1)} collective-permute-done((f32[256,256]{0,1:T(8,128)S(1)}, f32[256,256]{0,1:T(8,128)S(1)}, u32[]{:S(2)}, u32[]{:S(2)}) %collective-permute-start.6) | collective-permute-done | bytes 262176 | tf_op jit(solution)/shard_map/ppermute | solution.py:26
  274.7 3.1 collective-permute-start.9
  277.8 2.4 collective-permute-start.8
  280.2 25.4 %collective-permute-done.8 = f32[256,256]{0,1:T(8,128)S(1)} collective-permute-done((f32[256,256]{0,1:T(8,128)S(1)}, f32[256,256]{0,1:T(8,128)S(1)}, u32[]{:S(2)}, u32[]{:S(2)}) %collective-permute-start.8) | collective-permute-done | bytes 262176 | tf_op jit(solution)/shard_map/ppermute | solution.py:26
  309.0 4.6 %collective-permute-start.11 = (f32[256,1024]{1,0:T(8,128)S(1)}, f32[256,1024]{1,0:T(8,128)S(1)}, u32[]{:S(2)}, u32[]{:S(2)}) collective-permute-start(f32[256,1024]{1,0:T(8,128)S(1)} %subtract_select_fusion.1), channel_id=1, source_target_pairs={{0,256},{8,264},{16,272},{24,280},{32,288},{40,296},{48,304},{56,3... | collective-permute-start | bytes 3145736 | tf_op jit(solution)/shard_map/ppermute | solution.py:26
  313.6 2.2 collective-permute-start.10
  315.8 24.8 %collective-permute-done.10 = f32[256,256]{0,1:T(8,128)S(1)} collective-permute-done((f32[256,256]{0,1:T(8,128)S(1)}, f32[256,256]{0,1:T(8,128)S(1)}, u32[]{:S(2)}, u32[]{:S(2)}) %collective-permute-start.10) | collective-permute-done | bytes 262176 | tf_op jit(solution)/shard_map/ppermute | solution.py:26
  342.8 1.2 subtract_select_fusion
  344.1 1.5 pad_maximum_fusion
  (38 shorter events, 21.4 us)
Async XLA Ops:
  6.5 63.8 %copy-start.2 = (f32[512,1024]{1,0:T(8,128)S(1)}, f32[512,1024]{1,0:T(8,128)}, u32[]{:S(2)}) copy-start(f32[512,1024]{1,0:T(8,128)} %param.5) | copy-start | bytes 6291460
  6.5 63.8 %all-gather.2.cloned.1.call-start = ((), (), s32[]{:S(2)}) async-start(), calls=%async_computation | async-start | bytes 4423680 | tf_op jit(solution)/shard_map/all_gather | solution.py:15
  70.4 5.3 %copy-start.4 = (f32[256,3840]{1,0:T(8,128)S(1)}, f32[256,3840]{1,0:T(8,128)}, u32[]{:S(2)}) copy-start(f32[256,3840]{1,0:T(8,128)} %all-gather.2.cloned.1.call-done) | copy-start | bytes 11796484
  73.4 2.2 copy-start.3
  78.8 22.7 %collective-permute-start.1 = (f32[256,1024]{1,0:T(8,128)}, f32[256,1024]{1,0:T(8,128)}, u32[]{:S(2)}, u32[]{:S(2)}) collective-permute-start(f32[256,1024]{1,0:T(8,128)} %get-tuple-element.13), channel_id=1, source_target_pairs={{0,8},{8,0},{16,24},{24,16},{32,40},{40,32},{48,56},{56,48},{64,72... | collective-permute-start | bytes 3145736 | tf_op jit(solution)/shard_map/ppermute | solution.py:26
  95.8 5.7 %copy-start = (f32[256,6,256]{2,0,1:T(8,128)S(1)}, f32[256,6,256]{2,0,1:T(8,128)}, u32[]{:S(2)}) copy-start(f32[256,6,256]{2,0,1:T(8,128)} %copy.13) | copy-start | bytes 4718596
  97.9 4.7 %copy-start.1 = (f32[256,6,256]{2,0,1:T(8,128)S(1)}, f32[256,6,256]{2,0,1:T(8,128)}, u32[]{:S(2)}) copy-start(f32[256,6,256]{2,0,1:T(8,128)} %copy.11) | copy-start | bytes 4718596
  97.9 3.6 %collective-permute-start = (f32[256,256]{0,1:T(8,128)S(1)}, f32[256,256]{0,1:T(8,128)S(1)}, u32[]{:S(2)}, u32[]{:S(2)}) collective-permute-start(f32[256,256]{0,1:T(8,128)S(1)} %get-tuple-element.12), channel_id=1, source_target_pairs={{0,8},{8,0},{16,24},{24,16},{32,40},{40,32},{48,56},{56,48},{64,72... | collective-permute-start | bytes 786440 | tf_op jit(solution)/shard_map/ppermute | solution.py:26
  106.1 32.1 %collective-permute-start.3 = (f32[256,1024]{1,0:T(8,128)S(1)}, f32[256,1024]{1,0:T(8,128)S(1)}, u32[]{:S(2)}, u32[]{:S(2)}) collective-permute-start(f32[256,1024]{1,0:T(8,128)S(1)} %subtract_select_fusion.5), channel_id=1, source_target_pairs={{0,16},{8,24},{16,0},{24,8},{32,48},{40,56},{48,32},{56,40},{64,80... | collective-permute-start | bytes 3145736 | tf_op jit(solution)/shard_map/ppermute | solution.py:26
  109.4 28.8 %collective-permute-start.2 = (f32[256,256]{0,1:T(8,128)S(1)}, f32[256,256]{0,1:T(8,128)S(1)}, u32[]{:S(2)}, u32[]{:S(2)}) collective-permute-start(f32[256,256]{0,1:T(8,128)S(1)} %get-tuple-element.11), channel_id=1, source_target_pairs={{0,16},{8,24},{16,0},{24,8},{32,48},{40,56},{48,32},{56,40},{64,80... | collective-permute-start | bytes 786440 | tf_op jit(solution)/shard_map/ppermute | solution.py:26
  141.7 60.6 %collective-permute-start.5 = (f32[256,1024]{1,0:T(8,128)S(1)}, f32[256,1024]{1,0:T(8,128)S(1)}, u32[]{:S(2)}, u32[]{:S(2)}) collective-permute-start(f32[256,1024]{1,0:T(8,128)S(1)} %subtract_select_fusion.4), channel_id=1, source_target_pairs={{0,32},{8,40},{16,48},{24,56},{32,0},{40,8},{48,16},{56,24},{64,96... | collective-permute-start | bytes 3145736 | tf_op jit(solution)/shard_map/ppermute | solution.py:26
  146.0 56.2 %collective-permute-start.4 = (f32[256,256]{0,1:T(8,128)S(1)}, f32[256,256]{0,1:T(8,128)S(1)}, u32[]{:S(2)}, u32[]{:S(2)}) collective-permute-start(f32[256,256]{0,1:T(8,128)S(1)} %get-tuple-element.10), channel_id=1, source_target_pairs={{0,32},{8,40},{16,48},{24,56},{32,0},{40,8},{48,16},{56,24},{64,96... | collective-permute-start | bytes 786440 | tf_op jit(solution)/shard_map/ppermute | solution.py:26
  205.7 65.5 %collective-permute-start.7 = (f32[256,1024]{1,0:T(8,128)S(1)}, f32[256,1024]{1,0:T(8,128)S(1)}, u32[]{:S(2)}, u32[]{:S(2)}) collective-permute-start(f32[256,1024]{1,0:T(8,128)S(1)} %subtract_select_fusion.3), channel_id=1, source_target_pairs={{0,64},{8,72},{16,80},{24,88},{32,96},{40,104},{48,112},{56,120},{... | collective-permute-start | bytes 3145736 | tf_op jit(solution)/shard_map/ppermute | solution.py:26
  214.3 57.0 %collective-permute-start.6 = (f32[256,256]{0,1:T(8,128)S(1)}, f32[256,256]{0,1:T(8,128)S(1)}, u32[]{:S(2)}, u32[]{:S(2)}) collective-permute-start(f32[256,256]{0,1:T(8,128)S(1)} %get-tuple-element.9), channel_id=1, source_target_pairs={{0,64},{8,72},{16,80},{24,88},{32,96},{40,104},{48,112},{56,120},{... | collective-permute-start | bytes 786440 | tf_op jit(solution)/shard_map/ppermute | solution.py:26
  274.7 30.9 %collective-permute-start.9 = (f32[256,1024]{1,0:T(8,128)S(1)}, f32[256,1024]{1,0:T(8,128)S(1)}, u32[]{:S(2)}, u32[]{:S(2)}) collective-permute-start(f32[256,1024]{1,0:T(8,128)S(1)} %subtract_select_fusion.2), channel_id=1, source_target_pairs={{0,128},{8,136},{16,144},{24,152},{32,160},{40,168},{48,176},{56,1... | collective-permute-start | bytes 3145736 | tf_op jit(solution)/shard_map/ppermute | solution.py:26
  277.8 27.8 %collective-permute-start.8 = (f32[256,256]{0,1:T(8,128)S(1)}, f32[256,256]{0,1:T(8,128)S(1)}, u32[]{:S(2)}, u32[]{:S(2)}) collective-permute-start(f32[256,256]{0,1:T(8,128)S(1)} %get-tuple-element.8), channel_id=1, source_target_pairs={{0,128},{8,136},{16,144},{24,152},{32,160},{40,168},{48,176},{56,1... | collective-permute-start | bytes 786440 | tf_op jit(solution)/shard_map/ppermute | solution.py:26
  309.0 31.6 %collective-permute-start.11 = (f32[256,1024]{1,0:T(8,128)S(1)}, f32[256,1024]{1,0:T(8,128)S(1)}, u32[]{:S(2)}, u32[]{:S(2)}) collective-permute-start(f32[256,1024]{1,0:T(8,128)S(1)} %subtract_select_fusion.1), channel_id=1, source_target_pairs={{0,256},{8,264},{16,272},{24,280},{32,288},{40,296},{48,304},{56,3... | collective-permute-start | bytes 3145736 | tf_op jit(solution)/shard_map/ppermute | solution.py:26
  313.6 27.0 %collective-permute-start.10 = (f32[256,256]{0,1:T(8,128)S(1)}, f32[256,256]{0,1:T(8,128)S(1)}, u32[]{:S(2)}, u32[]{:S(2)}) collective-permute-start(f32[256,256]{0,1:T(8,128)S(1)} %get-tuple-element.7), channel_id=1, source_target_pairs={{0,256},{8,264},{16,272},{24,280},{32,288},{40,296},{48,304},{56,3... | collective-permute-start | bytes 786440 | tf_op jit(solution)/shard_map/ppermute | solution.py:26
Sparse Core Ops, SparseCore 0:
  10.4 59.9 all-gather.1
where the time goes:
time: 355 us; the launch traced here: 352 us
  waiting for transfers between devices  248 us (70%)
  starting transfers between devices  39.3 us (11%)
  matrix products  28.9 us (8%)
  local copies, waits for them, and re-layouts  17.5 us (5%)
  between operations  13.8 us (4%)
  other arithmetic  5.28 us (1%)
    ppermute x12, waiting for transfers between devices, swapped(): return lax.ppermute(value, axis, pairs)  188 us
    all_gather x1, waiting for transfers between devices, turned_gather(): whole, at, done = (lax.all_gather(both, axis, axis=0, tiled=True), 0, [])  59.9 us
    ppermute x12, starting transfers between devices, swapped(): return lax.ppermute(value, axis, pairs)  39.3 us
    dot_general x6, matrix products, combine(): coupling = jnp.einsum('kb,kc->bc', chosen_tri, summed, precision=highest)  8.21 us
    slice x3, local copies, waits for them, and re-layouts, turned_gather(): section = whole[:, at:at + t[0].size].reshape(-1, *t.shape[1:])  8.18 us
    dot_general x6, matrix products, combine(): jnp.einsum('bk,kc->bc', chosen_y, coupling, precision=highest)  7.11 us
  transfers between devices with their start and end apart: 13, of which 7 were waited for; matrix products, arithmetic and copies ran while one was open for 5% of the time, Pallas kernels for 0%

commit v1 on v0

v1 whole, which is shorter than its diff:
```python
import jax
import jax.numpy as jnp
from jax import lax
from jax.experimental import pallas as pl
from jax.experimental.pallas import tpu as pltpu
from jax.sharding import PartitionSpec as P

B = 256
S = 32
W = 128
MESH = pl.DeviceIdType.MESH
F32 = jnp.float32
BF16 = jnp.bfloat16


def rem(a, b):
    return lax.rem(a, jnp.int32(b))


def div(a, b):
    return lax.div(a, jnp.int32(b))


def swap(v):
    return rem(v, 2) * 2 + div(v, 2)


def split(x):
    hi = x.astype(BF16)
    lo = (x - hi.astype(F32)).astype(BF16)
    return hi, lo


def dot(a, b):
    return jnp.dot(a, b, preferred_element_type=F32)


def mul(stacked, x):
    hi, lo = split(x)
    both = dot(stacked[...], hi)
    return both[:B] + (both[B:] + dot(stacked[:B], lo))


def put(stacked, x):
    hi, lo = split(x)
    stacked[:B] = hi
    stacked[B:] = lo


def triangle(turned):
    row = lax.broadcasted_iota(jnp.int32, (B, B), 0)
    col = lax.broadcasted_iota(jnp.int32, (B, B), 1)
    kept = jnp.where(col <= row, turned, 0.0)
    return kept + jnp.where(col == row, 0.5, 0.0).astype(F32)


def kernel(
    tr, vh, th, nr, nf, out,
    VL, TL, PL, WS, LB, PB, A8, SND, SC, OB, X0, X1, X2, FIN,
    VT, VN, TT, FT, YT, YN,
    ld, lda, ring_s, ring_r, pg_s, pg_r, sib_s, sib_r, late_s, late_r, a_s, a_r, b_s, b_r, c_s, c_r, f_s, f_r, st,
):
    r = lax.axis_index("row")
    y = lax.axis_index("col")
    d0 = rem(r, 4)
    d1 = rem(div(r, 4), 4)
    d2 = div(r, 16)
    core = rem(d0, 2)
    z0 = div(d0, 2)

    def row(a, b, c):
        return a + 4 * b + 16 * c

    right = rem(y + 1, 8)
    left = rem(y + 7, 8)
    sibling = row(d0 + 1 - 2 * core, d1, d2)

    load_v = pltpu.make_async_copy(vh, VL, ld.at[0])
    load_t = pltpu.make_async_copy(th, TL, ld.at[1])
    load_v.start()
    load_t.start()
    bits = [rem(div(r, 1 << s), 2) for s in range(6)]
    for s in range(6):

        @pl.when(bits[s] == 0)
        def _():
            pltpu.make_async_copy(nf.at[s], PL.at[s], ld.at[2 + s]).start()

        @pl.when(bits[s] == 1)
        def _():
            pltpu.make_async_copy(nr.at[s], PL.at[s], ld.at[2 + s]).start()

    for c in range(8):
        pltpu.make_async_copy(tr.at[:, c * W : (c + 1) * W], A8.at[c], lda.at[c]).start()

    barrier = pltpu.get_barrier_semaphore()

    def greet(a, b):
        pl.semaphore_signal(barrier, inc=1, device_id=(a, b), device_id_type=MESH)

    greet(r, right)
    greet(r, left)
    for t in range(1, 4):
        greet(row(rem(d0 + t, 4), d1, d2), y)
        greet(row(d0, rem(d1 + t, 4), d2), y)
        greet(row(d0, d1, rem(d2 + t, 4)), y)
    self_b = d1 == swap(d0)
    back = rem(d2 - d1 + 4, 4)
    self_c = back == d1
    for t in range(4):
        if t:
            greet(row(swap(d1), rem(d1 + t, 4), d2), y)
            greet(row(d0, back, rem(d2 + t, 4)), y)
        else:

            @pl.when(jnp.logical_not(self_b))
            def _():
                greet(row(swap(d1), d1, d2), y)

            @pl.when(jnp.logical_not(self_c))
            def _():
                greet(row(d0, back, d2), y)

    mine = pl.ds(pl.multiple_of(y * S, S), S)
    load_v.wait()
    load_t.wait()
    LB[0, mine, :] = jnp.transpose(VL[:B, :])
    LB[1, mine, :] = jnp.transpose(VL[B:, :])
    LB[2, mine, :] = jnp.transpose(TL[...])

    expected = 2 + 9 + 6 + jnp.where(self_b, 0, 1) + jnp.where(self_c, 0, 1)
    pl.semaphore_wait(barrier, expected)

    def block(q, owner, half):
        start = owner * S + (16 if half == 1 else 0)
        rows = pl.ds(pl.multiple_of(start, 16), S if half is None else 16)
        if q == 0:
            return LB.at[:, rows, :]
        if q == 1:
            return PB.at[0, core, :, rows, :]
        if q == 2:
            return PB.at[1, :, :, rows, :]
        return PB.at[2, :, d2, rows, :]

    def ring(q, way, t):
        owner = rem(y + (8 - t if way == 0 else t), 8)
        ref = block(q, owner, way if t == 3 else None)
        return pltpu.make_async_remote_copy(
            ref, ref, ring_s.at[q, way, t], ring_r.at[q, way, t],
            device_id=(r, right if way == 0 else left), device_id_type=MESH,
        )

    def arrival(q, way, t):
        owner = rem(y + (7 - t if way == 0 else t + 1), 8)
        ref = block(q, owner, way if t == 3 else None)
        return ref, pltpu.make_async_remote_copy(
            ref, ref, ring_s.at[q, way, t], ring_r.at[q, way, t],
            device_id=(r, right if way == 0 else left), device_id_type=MESH,
        )

    def to_sibling(ref, n):
        return pltpu.make_async_remote_copy(
            ref, ref, sib_s.at[n], sib_r.at[n], device_id=(sibling, y), device_id_type=MESH,
        )

    def ring_begin(q):
        for way in range(2):
            ring(q, way, 0).start()
        if q == 1:
            to_sibling(block(1, y, None), 8).start()

    def ring_step(q, t):
        for way in range(2):
            ref, copy = arrival(q, way, t)
            copy.wait_recv()
            if t < 3:
                ring(q, way, t + 1).start()
            if q == 1:
                to_sibling(ref, 2 * t + way).start()

    ring_begin(0)

    for s in range(6):
        pltpu.make_async_copy(nf.at[s], PL.at[s], ld.at[2 + s]).wait()
        WS[s] = jnp.transpose(PL[s])

    def pre0(level, side):
        to = level + 2 * side
        return pltpu.make_async_remote_copy(
            WS.at[level], PB.at[0, level, d0, mine, :], pg_s.at[2 * level + side], pg_r.at[d0],
            device_id=(row(jnp.int32(to), d1, d2), y), device_id_type=MESH,
        )

    def pre0_own(level):
        return pltpu.make_async_copy(WS.at[level], PB.at[0, level, d0, mine, :], pg_r.at[d0])

    for level in range(2):
        for side in range(2):

            @pl.when(d0 != level + 2 * side)
            def _():
                pre0(level, side).start()

            @pl.when(d0 == level + 2 * side)
            def _():
                pre0_own(level).start()

    def pre1(t):
        return pltpu.make_async_remote_copy(
            WS.at[2:4], PB.at[1, :, d1, mine, :], pg_s.at[4 + t], pg_r.at[4 + d1],
            device_id=(row(d0, rem(d1 + t, 4), d2), y), device_id_type=MESH,
        )

    for t in (2, 1, 3):
        pre1(t).start()
    own1 = pltpu.make_async_copy(WS.at[2:4], PB.at[1, :, d1, mine, :], pg_r.at[4 + d1])
    own1.start()
    own2 = pltpu.make_async_copy(WS.at[4:6], PB.at[2, :, d2, mine, :], pg_r.at[8])
    own2.start()

    def pre0_wait():
        for j in range(4):
            pltpu.make_async_copy(WS.at[0], PB.at[0, core, j, mine, :], pg_r.at[j]).wait()

    def pre1_wait():
        for j in range(4):
            pltpu.make_async_copy(WS.at[2:4], PB.at[1, :, j, mine, :], pg_r.at[4 + j]).wait()

    ring_step(0, 0)
    ring_step(0, 1)
    pre0_wait()
    ring_begin(1)
    ring_step(0, 2)
    ring_step(0, 3)

    for n in range(2):
        flat = LB[n]
        put(VT.at[n], flat)
        put(VN.at[n], jnp.transpose(flat))
    put(TT, triangle(LB[2]))
    ring_step(1, 0)

    def spread(k):
        other = 2 - 2 * z0
        return jnp.where(
            k == 0, other + core, jnp.where(k == 1, other + 1 - core, jnp.where(k == 2, 2 * z0 + 1 - core, d0))
        )

    def a_copy(h, k):
        to = spread(k)
        chunk = 2 * to + h
        return pltpu.make_async_remote_copy(
            SND.at[chunk], X0.at[h, d0], a_s.at[h, k], a_r.at[h, d0],
            device_id=(row(to, d1, d2), y), device_id_type=MESH,
        )

    def leaf(h):
        def body(k, _):
            chunk = 2 * spread(k) + h
            pltpu.make_async_copy(tr.at[:, 0:W], A8.at[chunk], lda.at[chunk]).wait()
            upper = A8[chunk, :B, :]
            lower = A8[chunk, B:, :]
            inner = mul(VT.at[0], upper) + mul(VT.at[1], lower)
            scaled = mul(TT, inner)
            SC[chunk] = scaled
            SND[chunk] = upper - mul(VN.at[0], scaled)

            @pl.when(k < 3)
            def _():
                a_copy(h, k).start()

            @pl.when(k == 3)
            def _():
                pltpu.make_async_copy(SND.at[chunk], X0.at[h, d0], a_r.at[h, d0]).start()

            return 0

        lax.fori_loop(0, 4, body, 0)

    leaf(0)
    ring_step(1, 1)
    leaf(1)
    ring_step(1, 2)
    pre1_wait()
    ring_begin(2)

    def remainder(chunk, _):
        OB[chunk] = A8[chunk, B:, :] - mul(VN.at[1], SC[chunk])
        pltpu.make_async_copy(
            OB.at[chunk], out.at[B:, pl.ds(pl.multiple_of(chunk * W, W), W)], st.at[chunk]
        ).start()
        return 0

    lax.fori_loop(0, 8, remainder, 0)
    ring_step(1, 3)
    own2.wait()

    def sibling_wait():
        other = PB.at[0, 1 - core]
        for n in range(8):
            way, t = n % 2, n // 2
            owner = rem(y + (7 - t if way == 0 else t + 1), 8)
            start = owner * S + (16 if t == 3 and way == 1 else 0)
            rows = pl.ds(pl.multiple_of(start, 16), S if t < 3 else 16)
            ref = other.at[:, rows, :]
            to_sibling(ref, n).wait_recv()
        to_sibling(other.at[:, mine, :], 8).wait_recv()

    def prepare(q):
        def body(e, _):
            level, n = div(e, 2), rem(e, 2)
            k = (2 - level) * n
            p = k + 1 + level
            put(FT.at[e], triangle(PB[q, level, k]))
            turned = PB[q, level, p]
            put(YT.at[e], turned)
            put(YN.at[e], jnp.transpose(turned))
            return 0

        lax.fori_loop(0, 4, body, 0)

    def apply(X, h):
        def body(level, _):
            at = [((2 - level) * n, (2 - level) * n + 1 + level) for n in range(2)]
            for n in range(2):
                k, p = at[n]
                e = 2 * level + n
                lead = X[h, k]
                follow = X[h, p]
                summed = lead + mul(YT.at[e], follow)
                coupling = mul(FT.at[e], summed)
                X[h, k] = lead - coupling
                X[h, p] = follow - mul(YN.at[e], coupling)
            return 0

        lax.fori_loop(0, 2, body, 0)

    def tops_wait(X, sem, h):
        for j in range(4):
            pltpu.make_async_copy(X.at[h, j], X.at[h, j], sem.at[h, j]).wait()

    def b_copy(h, t):
        i = rem(d0 + t, 4)
        return pltpu.make_async_remote_copy(
            X0.at[h, i], X1.at[h, d1], b_s.at[h, t], b_r.at[h, d1],
            device_id=(row(i, swap(d0), d2), y), device_id_type=MESH,
        )

    def c_copy(h, t):
        i = rem(d1 + t, 4)
        return pltpu.make_async_remote_copy(
            X1.at[h, i], X2.at[h, d2], c_s.at[h, t], c_r.at[h, d2],
            device_id=(row(d0, i, rem(d1 + i, 4)), y), device_id_type=MESH,
        )

    to_self_c = rem(d1 + d1, 4) == d2

    def f_copy(h, t):
        i = rem(d2 + t, 4)
        return pltpu.make_async_remote_copy(
            X2.at[h, i], FIN.at[h, d2], f_s.at[h, t], f_r.at[h, d2],
            device_id=(row(d0, d1, i), y), device_id_type=MESH,
        )

    def send(copy, h, own, local):
        for t in (2, 1, 3):
            copy(h, t).start()
        if own is None:
            local.start()
        else:

            @pl.when(jnp.logical_not(own))
            def _():
                copy(h, 0).start()

            @pl.when(own)
            def _():
                local.start()

    sibling_wait()
    prepare(0)
    ring_step(2, 0)
    for h in range(2):
        tops_wait(X0, a_r, h)
        apply(X0, h)
        send(b_copy, h, self_b, pltpu.make_async_copy(X0.at[h, d0], X1.at[h, d1], b_r.at[h, d1]))
        if h == 0:
            ring_step(2, 1)
            ring_begin(3)
    ring_step(2, 2)
    ring_step(2, 3)
    prepare(1)
    for t in range(3):
        ring_step(3, t)

    def late(t):
        return pltpu.make_async_remote_copy(
            PB.at[2, :, d2], PB.at[2, :, d2], late_s.at[t], late_r.at[d2],
            device_id=(row(d0, d1, rem(d2 + t, 4)), y), device_id_type=MESH,
        )

    for h in range(2):
        tops_wait(X1, b_r, h)
        apply(X1, h)
        send(c_copy, h, to_self_c, pltpu.make_async_copy(X1.at[h, d1], X2.at[h, d2], c_r.at[h, d2]))
        if h == 0:
            ring_step(3, 3)
            for t in (2, 1, 3):
                late(t).start()

    for t in range(1, 4):
        j = rem(d2 + t, 4)
        pltpu.make_async_copy(PB.at[2, :, j], PB.at[2, :, j], late_r.at[j]).wait()
    prepare(2)

    for h in range(2):
        tops_wait(X2, c_r, h)
        apply(X2, h)
        send(f_copy, h, None, pltpu.make_async_copy(X2.at[h, d2], FIN.at[h, d2], f_r.at[h, d2]))

    def home(h, j):
        quarter = swap(rem(j - d1 + 4, 4))
        cols = pl.ds(pl.multiple_of(quarter * 256 + h * W, W), W)
        return pltpu.make_async_copy(FIN.at[h, j], out.at[:B, cols], st.at[8 + 4 * h + j])

    for h in range(2):
        for j in range(4):
            pltpu.make_async_copy(FIN.at[h, j], FIN.at[h, j], f_r.at[h, j]).wait()
            home(h, j).start()

    for q in range(4):
        for way in range(2):
            for t in range(4):
                ring(q, way, t).wait_send()
    for n in range(8):
        ref, _ = arrival(1, n % 2, n // 2)
        to_sibling(ref, n).wait_send()
    to_sibling(block(1, y, None), 8).wait_send()
    for level in range(2):
        for side in range(2):

            @pl.when(d0 != level + 2 * side)
            def _():
                pre0(level, side).wait_send()

    for t in range(1, 4):
        pre1(t).wait_send()
        late(t).wait_send()
    for h in range(2):
        for k in range(3):
            a_copy(h, k).wait_send()
        for t in range(1, 4):
            b_copy(h, t).wait_send()
            c_copy(h, t).wait_send()
            f_copy(h, t).wait_send()

        @pl.when(jnp.logical_not(self_b))
        def _():
            b_copy(h, 0).wait_send()

        @pl.when(jnp.logical_not(to_self_c))
        def _():
            c_copy(h, 0).wait_send()

    for chunk in range(8):
        pltpu.make_async_copy(OB.at[chunk], out.at[B:, chunk * W : (chunk + 1) * W], st.at[chunk]).wait()
    for h in range(2):
        for j in range(4):
            home(h, j).wait()


def per_device(trailing, reflectors, leaf_factor, node_reflect, node_factor):
    anywhere = pl.BlockSpec(memory_space=pl.ANY)
    dma = pltpu.SemaphoreType.DMA
    tops = pltpu.VMEM((2, 4, B, W), F32)
    nodes = pltpu.VMEM((4, 2 * B, B), BF16)
    return pl.pallas_call(
        kernel,
        out_shape=jax.ShapeDtypeStruct(trailing.shape, F32),
        in_specs=[anywhere] * 5,
        out_specs=anywhere,
        scratch_shapes=[
            pltpu.VMEM((2 * B, S), F32),
            pltpu.VMEM((B, S), F32),
            pltpu.VMEM((6, B, S), F32),
            pltpu.VMEM((6, S, B), F32),
            pltpu.VMEM((3, B, B), F32),
            pltpu.VMEM((3, 2, 4, B, B), F32),
            pltpu.VMEM((8, 2 * B, W), F32),
            pltpu.VMEM((8, B, W), F32),
            pltpu.VMEM((8, B, W), F32),
            pltpu.VMEM((8, B, W), F32),
            tops, tops, tops, tops,
            pltpu.VMEM((2, 2 * B, B), BF16),
            pltpu.VMEM((2, 2 * B, B), BF16),
            pltpu.VMEM((2 * B, B), BF16),
            nodes, nodes, nodes,
            dma((8,)), dma((8,)),
            dma((4, 2, 4)), dma((4, 2, 4)),
            dma((8,)), dma((9,)),
            dma((9,)), dma((9,)),
            dma((4,)), dma((4,)),
            dma((2, 4)), dma((2, 4)),
            dma((2, 4)), dma((2, 4)),
            dma((2, 4)), dma((2, 4)),
            dma((2, 4)), dma((2, 4)),
            dma((16,)),
        ],
        compiler_params=pltpu.CompilerParams(
            collective_id=0, has_side_effects=True, vmem_limit_bytes=56 * 1024 * 1024
        ),
        name="update",
    )(trailing, reflectors, leaf_factor, node_reflect, node_factor)


def solution(mesh):
    in_specs = (
        P("row", "col"),
        P("row", "col"),
        P("row", "col"),
        P(None, "row", "col"),
        P(None, "row", "col"),
    )
    return jax.shard_map(
        per_device, mesh=mesh, in_specs=in_specs, out_specs=P("row", "col"), check_vma=False
    )
```

time: 355 us -> 144 us (0.41)
  waiting for transfers between devices: 248 us -> 0 us
  Pallas kernels: 0 us -> 133 us
  starting transfers between devices: 39.3 us -> 0 us
  matrix products: 28.9 us -> 0 us
  between operations: 13.8 us -> 0.01 us
  local copies, waits for them, and re-layouts: 17.5 us -> 10.5 us
  other arithmetic: 5.28 us -> 0 us
    ppermute x12 -> x0, waiting for transfers between devices: 188 us -> none  [swapped(): return lax.ppermute(value, axis, pairs)]
    pallas_call x0 -> x1, Pallas kernels: none -> 133 us  [per_device(): pl.pallas_call(kernel, out_shape=jax.ShapeDtypeStruct(trailing.shape, F32...]
    all_gather x1 -> x0, waiting for transfers between devices: 59.9 us -> none  [turned_gather(): whole, at, done = (lax.all_gather(both, axis, axis=0, tiled=True), 0, [])]
    ppermute x12 -> x0, starting transfers between devices: 39.3 us -> none  [swapped(): return lax.ppermute(value, axis, pairs)]
    dot_general x21 -> x0, matrix products: 28.9 us -> none  [the longest x6 8.21 us: combine(): coupling = jnp.einsum('kb,kc->bc', chosen_tri, summed, precision=highest)]
    unnamed x10 -> x5, local copies, waits for them, and re-layouts: 0.02 us -> 10.5 us
    slice x4 -> x0, local copies, waits for them, and re-layouts: 9.38 us -> none  [the longest x3 8.18 us: turned_gather(): section = whole[:, at:at + t[0].size].reshape(-1, *t.shape[1:])]
    reshape x4 -> x0, local copies, waits for them, and re-layouts: 8.09 us -> none  [the longest x2 6.06 us: turned_gather(): section = whole[:, at:at + t[0].size].reshape(-1, *t.shape[1:])]
  transfers between devices with their start and end apart: 13 -> 0, of which waited for: 7 -> 0; matrix products, arithmetic and copies ran while one was open for 5% -> 0% of each run, Pallas kernels for 0% -> 0%
where the time goes in v1:
time: 144 us; the launch traced here: 143 us
  Pallas kernels  133 us (92%)
  local copies, waits for them, and re-layouts  10.5 us (7%)
    pallas_call x1, Pallas kernels, per_device(): pl.pallas_call(kernel, out_shape=jax.ShapeDtypeStruct(trailing.shape, F32...  133 us
    unnamed x5, local copies, waits for them, and re-layouts  10.5 us

profile of v1, /device:TPU:1, one launch (start us, length us, event | category | flops | bytes accessed | tf_op | source)
XLA Modules:
  0.0 143.1 jit_solution(7817869076301697958)
XLA Ops:
  0.0 1.5 %copy.7.th = f32[256,32]{1,0:T(8,128)} copy(f32[256,32]{0,1:T(8,128)} %param.7) | data formatting | bytes 65536 | tf_op args[2]
  1.5 1.7 %copy.6.vh = f32[512,32]{1,0:T(8,128)} copy(f32[512,32]{0,1:T(8,128)} %param.6) | data formatting | bytes 131072 | tf_op args[1]
  3.2 2.1 %copy.8.nr = f32[6,256,32]{2,1,0:T(8,128)} copy(f32[6,256,32]{1,2,0:T(8,128)} %param.8) | data formatting | bytes 393216 | tf_op args[3]
  5.3 2.1 %copy.9.nf = f32[6,256,32]{2,1,0:T(8,128)} copy(f32[6,256,32]{1,2,0:T(8,128)} %param.9) | data formatting | bytes 393216 | tf_op args[4]
  7.4 132.6 %update.1 = f32[512,1024]{1,0:T(8,128)} custom-call(f32[512,1024]{1,0:T(8,128)} %tr.1, f32[512,32]{1,0:T(8,128)} %copy.6.vh, f32[256,32]{1,0:T(8,128)} %copy.7.th, f32[6,256,32]{2,1,0:T(8,128)} %copy.8.nr, f32[6,256,32]{2,1,0:T(8,128)} %copy.9.nf), custom_call_target="tpu_custom_call" | custom-call | tf_op jit(solution)/shard_map/update/pallas_call | solution.py:477
  140.0 3.2 %copy.11 = f32[512,1024]{1,0:T(8,128)} copy(f32[512,1024]{1,0:T(8,128)} %update.1) | data formatting | bytes 4194304

commit v2 on v1

v2 whole, which is shorter than its diff:
```python
import jax
import jax.numpy as jnp
from jax import lax
from jax.experimental import pallas as pl
from jax.experimental.pallas import tpu as pltpu
from jax.sharding import PartitionSpec as P

B = 256
S = 32
W = 128
SHARED = (3, 4, 6, 7)
MESH = pl.DeviceIdType.MESH
F32 = jnp.float32
BF16 = jnp.bfloat16


def rem(a, b):
    return lax.rem(a, jnp.int32(b))


def div(a, b):
    return lax.div(a, jnp.int32(b))


def split(x):
    hi = x.astype(BF16)
    lo = (x - hi.astype(F32)).astype(BF16)
    return hi, lo


def dot(a, b):
    return jnp.dot(a, b, preferred_element_type=F32)


def mul(stacked, x):
    hi, lo = split(x)
    both = dot(stacked[...], hi)
    return both[:B] + (both[B:] + dot(stacked[:B], lo))


def narrow(stacked, x):
    both = dot(stacked[...], jnp.concatenate(split(x), axis=1))
    return both[:B, :W] + (both[:B, W:] + both[B:, :W])


def put(stacked, x):
    hi, lo = split(x)
    stacked[:B] = hi
    stacked[B:] = lo


def triangle(turned):
    row = lax.broadcasted_iota(jnp.int32, (B, B), 0)
    col = lax.broadcasted_iota(jnp.int32, (B, B), 1)
    kept = jnp.where(col <= row, turned, 0.0)
    return kept + jnp.where(col == row, 0.5, 0.0).astype(F32)


def kernel(
    tr, vh, th, nr, nf, top_out, low_out,
    WS, LB, PB, A4, SND, SC, OB, X0, X1, X2,
    VT, VN, TT, FT, YT, YN,
    ld, lda, ring_s, ring_r, pg_s, pg_r, sib_s, sib_r, late_s, late_r, top_s, top_r, st,
):
    r = lax.axis_index("row")
    y = lax.axis_index("col")
    d0 = rem(r, 4)
    d1 = rem(div(r, 4), 4)
    d2 = div(r, 16)
    core = rem(d0, 2)
    z0 = div(d0, 2)
    z1 = rem(d1, 2)
    z2 = div(d1, 2)

    def row(a, b, c):
        return a + 4 * b + 16 * c

    right = rem(y + 1, 8)
    left = rem(y + 7, 8)
    sibling = row(d0 + 1 - 2 * core, d1, d2)

    mine = pl.ds(pl.multiple_of(y * S, S), S)

    pltpu.make_async_copy(vh.at[:, :B], LB.at[0, mine, :], ld.at[0]).start()
    pltpu.make_async_copy(vh.at[:, B:], LB.at[1, mine, :], ld.at[0]).start()
    pltpu.make_async_copy(th, LB.at[2, mine, :], ld.at[0]).start()
    bits = [rem(div(r, 1 << s), 2) for s in range(6)]
    for s in range(6):

        @pl.when(bits[s] == 0)
        def _():
            pltpu.make_async_copy(nf.at[s], WS.at[s], ld.at[1]).start()

        @pl.when(bits[s] == 1)
        def _():
            pltpu.make_async_copy(nr.at[s], WS.at[s], ld.at[1]).start()

    for c in range(4):
        pltpu.make_async_copy(tr.at[:, c * B : (c + 1) * B], A4.at[c], lda.at[c]).start()

    barrier = pltpu.get_barrier_semaphore()

    def greet(a, b):
        pl.semaphore_signal(barrier, inc=1, device_id=(a, b), device_id_type=MESH)

    greet(r, right)
    greet(r, left)
    for t in range(1, 4):
        greet(row(rem(d0 + t, 4), d1, d2), y)
        greet(row(d0, d1, rem(d2 + t, 4)), y)
    held = rem(d2 - d1 + 4, 4)
    self_a = z2 == core
    self_b = z1 == z0
    self_c = jnp.logical_and(self_a, held == core + 2 * z1)
    for t in range(4):
        sources = (
            (self_a, row(z2 + 2 * z0, rem(d1 + t, 4), d2)),
            (self_b, row(core + 2 * z1, rem(d1 + t, 4), d2)),
            (self_c, row(rem(held, 2) + 2 * z0, div(held, 2) + 2 * core, rem(d2 + t, 4))),
        )
        for own, source in sources:
            if t:
                greet(source, y)
            else:

                @pl.when(jnp.logical_not(own))
                def _():
                    greet(source, y)

    def arrived(ref, sem):
        pltpu.make_async_copy(ref, ref, sem).wait()

    arrived(LB.at[:, mine, :], ld.at[0])
    expected = 8 + 9
    for own in (self_a, self_b, self_c):
        expected = expected + jnp.where(own, 0, 1)
    pl.semaphore_wait(barrier, expected)

    def block(q, owner, half):
        start = owner * S + (16 if half == 1 else 0)
        rows = pl.ds(pl.multiple_of(start, 16), S if half is None else 16)
        if q < 3:
            return LB.at[q, rows, :]
        if q < 5:
            return PB.at[0, core, 2 * (q - 3) : 2 * (q - 2), rows, :]
        if q == 5:
            return PB.at[2, :, d2, rows, :]
        return PB.at[1, core, 2 * (q - 6) : 2 * (q - 5), rows, :]

    def ring(q, way, t):
        owner = rem(y + (8 - t if way == 0 else t), 8)
        ref = block(q, owner, way if t == 3 else None)
        return pltpu.make_async_remote_copy(
            ref, ref, ring_s.at[q], ring_r.at[q, way, t],
            device_id=(r, right if way == 0 else left), device_id_type=MESH,
        )

    def arrival(q, way, t):
        owner = rem(y + (7 - t if way == 0 else t + 1), 8)
        ref = block(q, owner, way if t == 3 else None)
        return ref

    def to_sibling(ref, q):
        return pltpu.make_async_remote_copy(
            ref, ref, sib_s.at[q], sib_r.at[q], device_id=(sibling, y), device_id_type=MESH,
        )

    def ring_begin(q):
        for way in range(2):
            ring(q, way, 0).start()
        if q in SHARED:
            to_sibling(block(q, y, None), q).start()

    def ring_step(q, t):
        for way in range(2):
            ref = arrival(q, way, t)
            arrived(ref, ring_r.at[q, way, t])
            if t < 3:
                ring(q, way, t + 1).start()
            if q in SHARED:
                to_sibling(ref, q).start()

    for q in range(3):
        ring_begin(q)
    arrived(WS, ld.at[1])

    def pre0(level, side):
        to = level + 2 * side
        return pltpu.make_async_remote_copy(
            WS.at[level], PB.at[0, level, d0, mine, :], pg_s.at[0], pg_r.at[0],
            device_id=(row(jnp.int32(to), d1, d2), y), device_id_type=MESH,
        )

    def pre0_own(level):
        return pltpu.make_async_copy(WS.at[level], PB.at[0, level, d0, mine, :], pg_r.at[0])

    for level in range(2):
        for side in range(2):

            @pl.when(d0 != level + 2 * side)
            def _():
                pre0(level, side).start()

            @pl.when(d0 == level + 2 * side)
            def _():
                pre0_own(level).start()

    def pre1(level, side):
        return pltpu.make_async_remote_copy(
            WS.at[2 + level], PB.at[1, level, d1, mine, :], pg_s.at[1], pg_r.at[1],
            device_id=(row(level + 2 * z0, side + 2 * core, d2), y), device_id_type=MESH,
        )

    def pre1_own(level, side):
        return jnp.logical_and(self_a, jnp.logical_and(core == level, z1 == side))

    for level in range(2):
        for side in range(2):

            @pl.when(jnp.logical_not(pre1_own(level, side)))
            def _():
                pre1(level, side).start()

            @pl.when(pre1_own(level, side))
            def _():
                pltpu.make_async_copy(WS.at[2 + level], PB.at[1, level, d1, mine, :], pg_r.at[1]).start()

    own2 = pltpu.make_async_copy(WS.at[4:6], PB.at[2, :, d2, mine, :], pg_r.at[2])
    own2.start()

    for t in range(2):
        for q in range(3):
            ring_step(q, t)
    arrived(PB.at[0, core, :, mine, :], pg_r.at[0])
    for q in range(3):
        ring_step(q, 2)
    ring_begin(3)
    ring_begin(4)
    own2.wait()
    ring_begin(5)
    for n in range(2):
        ring_step(n, 3)
        flat = LB[n]
        put(VT.at[n], flat)
        put(VN.at[n], jnp.transpose(flat))
    ring_step(2, 3)
    put(TT, triangle(LB[2]))

    def spread(k):
        other = 2 - 2 * z0
        return jnp.where(
            k == 0, other + core, jnp.where(k == 1, other + 1 - core, jnp.where(k == 2, 2 * z0 + 1 - core, d0))
        )

    def a_copy(h, k):
        to = spread(k)
        return pltpu.make_async_remote_copy(
            SND.at[to, h], X0.at[h, d0], top_s.at[0], top_r.at[0, h],
            device_id=(row(to, d1, d2), y), device_id_type=MESH,
        )

    def leaf(pair, _):
        quarters = [spread(2 * pair), spread(2 * pair + 1)]
        for quarter in quarters:
            pltpu.make_async_copy(tr.at[:, 0:B], A4.at[quarter], lda.at[quarter]).wait()
        scaled = []
        for quarter in quarters:
            inner = mul(VT.at[0], A4[quarter, :B, :]) + mul(VT.at[1], A4[quarter, B:, :])
            scaled.append(mul(TT, inner))
        for quarter, value in zip(quarters, scaled):
            SC[quarter] = value
            leafed = A4[quarter, :B, :] - mul(VN.at[0], value)
            SND[quarter, 0] = leafed[:, :W]
            SND[quarter, 1] = leafed[:, W:]
        for h in range(2):
            a_copy(h, 2 * pair).start()

            @pl.when(pair == 0)
            def _():
                a_copy(h, 2 * pair + 1).start()

            @pl.when(pair == 1)
            def _():
                pltpu.make_async_copy(SND.at[d0, h], X0.at[h, d0], top_r.at[0, h]).start()

        return 0

    def remainder(quarter, _):
        OB[quarter] = A4[quarter, B:, :] - mul(VN.at[1], SC[quarter])
        pltpu.make_async_copy(
            OB.at[quarter], low_out.at[:, pl.ds(pl.multiple_of(quarter * B, B), B)], st
        ).start()
        return 0

    lax.fori_loop(0, 1, leaf, 0)
    ring_step(3, 0)
    ring_step(4, 0)
    lax.fori_loop(1, 2, leaf, 0)
    ring_step(3, 1)
    ring_step(4, 1)
    ring_step(5, 0)
    lax.fori_loop(0, 1, remainder, 0)
    ring_step(3, 2)
    ring_step(4, 2)
    ring_step(5, 1)
    arrived(PB.at[1, core, :, mine, :], pg_r.at[1])
    ring_begin(6)
    ring_step(3, 3)
    ring_step(4, 3)
    ring_step(5, 2)
    ring_begin(7)

    def sibling_wait(phase):
        for part in range(2):
            arrived(PB.at[phase, 1 - core, 2 * part : 2 * part + 2], sib_r.at[SHARED[2 * phase + part]])

    def prepare(q):
        def body(e, _):
            level, n = div(e, 2), rem(e, 2)
            k = (2 - level) * n
            p = k + 1 + level
            put(FT.at[e], triangle(PB[q, level, k]))
            turned = PB[q, level, p]
            put(YT.at[e], turned)
            put(YN.at[e], jnp.transpose(turned))
            return 0

        lax.fori_loop(0, 4, body, 0)

    def apply(X, h):
        def body(level, _):
            at = [((2 - level) * n, (2 - level) * n + 1 + level) for n in range(2)]
            for n in range(2):
                k, p = at[n]
                e = 2 * level + n
                lead = X[h, k]
                follow = X[h, p]
                summed = lead + narrow(YT.at[e], follow)
                coupling = narrow(FT.at[e], summed)
                X[h, k] = lead - coupling
                X[h, p] = follow - narrow(YN.at[e], coupling)
            return 0

        lax.fori_loop(0, 2, body, 0)

    kept_b = z2 + 2 * z0

    def b_copy(h, t):
        i = rem(kept_b + t, 4)
        return pltpu.make_async_remote_copy(
            X0.at[h, i], X1.at[h, d1], top_s.at[1], top_r.at[1, h],
            device_id=(row(core + 2 * div(i, 2), z0 + 2 * rem(i, 2), d2), y), device_id_type=MESH,
        )

    def c_copy(h, t):
        i = rem(d1 + t, 4)
        return pltpu.make_async_remote_copy(
            X1.at[h, i], X2.at[h, d2], top_s.at[2], top_r.at[2, h],
            device_id=(row(z2 + 2 * z0, i, rem(core + 2 * z1 + i, 4)), y), device_id_type=MESH,
        )

    def home(h):
        quarter = rem(d2 - d1 + 4, 4)
        return top_out.at[:, pl.ds(pl.multiple_of(quarter * B + h * W, W), W)]

    def f_copy(h, t):
        i = rem(d2 + t, 4)
        return pltpu.make_async_remote_copy(
            X2.at[h, i], home(h), top_s.at[3], top_r.at[3, h],
            device_id=(row(d0, d1, i), y), device_id_type=MESH,
        )

    def send(copy, h, own, local):
        for t in (2, 1, 3):
            copy(h, t).start()
        if own is None:
            local().start()
        else:

            @pl.when(jnp.logical_not(own))
            def _():
                copy(h, 0).start()

            @pl.when(own)
            def _():
                local().start()

    def late(t):
        return pltpu.make_async_remote_copy(
            PB.at[2, :, d2], PB.at[2, :, d2], late_s, late_r,
            device_id=(row(d0, d1, rem(d2 + t, 4)), y), device_id_type=MESH,
        )

    sibling_wait(0)
    prepare(0)
    for h in range(2):
        arrived(X0.at[h], top_r.at[0, h])
        apply(X0, h)
        send(b_copy, h, self_b, lambda: pltpu.make_async_copy(X0.at[h, kept_b], X1.at[h, d1], top_r.at[1, h]))
        if h == 0:
            ring_step(5, 3)
            for t in (2, 1, 3):
                late(t).start()
            ring_step(6, 0)
            ring_step(7, 0)
    ring_step(6, 1)
    ring_step(7, 1)
    lax.fori_loop(1, 4, remainder, 0)
    ring_step(6, 2)
    ring_step(7, 2)
    ring_step(6, 3)
    ring_step(7, 3)
    sibling_wait(1)
    prepare(1)


    for h in range(2):
        arrived(X1.at[h], top_r.at[1, h])
        apply(X1, h)
        send(c_copy, h, self_c, lambda: pltpu.make_async_copy(X1.at[h, d1], X2.at[h, d2], top_r.at[2, h]))

    arrived(PB.at[2, :, 0:3], late_r)
    prepare(2)

    for h in range(2):
        arrived(X2.at[h], top_r.at[2, h])
        apply(X2, h)
        send(f_copy, h, None, lambda: pltpu.make_async_copy(X2.at[h, d2], home(h), top_r.at[3, h]))

    for h in range(2):
        arrived(top_out.at[:, 0 : 4 * W], top_r.at[3, h])

    for q in range(8):
        rows = pl.ds(0, 7 * S)
        arrived(LB.at[q, rows] if q < 3 else PB.at[0, 0, 0:2, rows], ring_s.at[q])
    for q in SHARED:
        arrived(PB.at[0, 0, 0:2], sib_s.at[q])
    arrived(WS.at[0:3], pg_s.at[0])
    arrived(PB.at[2, :, 0:3], late_s)
    arrived(X0.at[:, 0:3], top_s.at[0])
    arrived(X0.at[:, 0:3], top_s.at[3])
    for own, sem, few, all_ in (
        (self_a, pg_s.at[1], WS.at[0:3], WS.at[0:4]),
        (self_b, top_s.at[1], X0.at[:, 0:3], X0),
        (self_c, top_s.at[2], X1.at[:, 0:3], X1),
    ):

        @pl.when(own)
        def _():
            arrived(few, sem)

        @pl.when(jnp.logical_not(own))
        def _():
            arrived(all_, sem)

    arrived(OB, st)


def per_device(trailing, reflectors, leaf_factor, node_reflect, node_factor):
    anywhere = pl.BlockSpec(memory_space=pl.ANY)
    dma = pltpu.SemaphoreType.DMA
    tops = pltpu.VMEM((2, 4, B, W), F32)
    nodes = pltpu.VMEM((4, 2 * B, B), BF16)
    half = jax.ShapeDtypeStruct((B, trailing.shape[1]), F32)
    top, low = pl.pallas_call(
        kernel,
        out_shape=(half, half),
        in_specs=[anywhere] * 5,
        out_specs=(anywhere, anywhere),
        scratch_shapes=[
            pltpu.VMEM((6, S, B), F32),
            pltpu.VMEM((3, B, B), F32),
            pltpu.VMEM((3, 2, 4, B, B), F32),
            pltpu.VMEM((4, 2 * B, B), F32),
            pltpu.VMEM((4, 2, B, W), F32),
            pltpu.VMEM((4, B, B), F32),
            pltpu.VMEM((4, B, B), F32),
            tops, tops, tops,
            pltpu.VMEM((2, 2 * B, B), BF16),
            pltpu.VMEM((2, 2 * B, B), BF16),
            pltpu.VMEM((2 * B, B), BF16),
            nodes, nodes, nodes,
            dma((2,)), dma((4,)),
            dma((8,)), dma((8, 2, 4)),
            dma((2,)), dma((3,)),
            dma((8,)), dma((8,)),
            dma, dma,
            dma((4,)), dma((4, 2)),
            dma,
        ],
        compiler_params=pltpu.CompilerParams(
            collective_id=0, has_side_effects=True, vmem_limit_bytes=56 * 1024 * 1024
        ),
        name="update",
    )(
        trailing,
        reflectors.T,
        leaf_factor.T,
        jnp.swapaxes(node_reflect, 1, 2),
        jnp.swapaxes(node_factor, 1, 2),
    )
    return jnp.concatenate([top, low], axis=0)


def solution(mesh):
    in_specs = (
        P("row", "col"),
        P("row", "col"),
        P("row", "col"),
        P(None, "row", "col"),
        P(None, "row", "col"),
    )
    return jax.shard_map(
        per_device, mesh=mesh, in_specs=in_specs, out_specs=P("row", "col"), check_vma=False
    )
```

time: 144 us -> 114 us (0.79)
  Pallas kernels: 133 us -> 110 us
  local copies, waits for them, and re-layouts: 10.5 us -> 0 us
  other arithmetic: 0 us -> 3.11 us
    pallas_call x1, Pallas kernels: 133 us -> 110 us  [per_device(): pl.pallas_call(kernel, out_shape=(half, half), in_specs=[anywhere] * 5, o...]
    unnamed x5 -> x0, local copies, waits for them, and re-layouts: 10.5 us -> none
    concatenate x0 -> x1, other arithmetic: none -> 3.11 us  [per_device(): return jnp.concatenate([top, low], axis=0)]
where the time goes in v2:
time: 114 us; the launch traced here: 113 us
  Pallas kernels  110 us (96%)
  other arithmetic  3.11 us (3%)
    pallas_call x1, Pallas kernels, per_device(): pl.pallas_call(kernel, out_shape=(half, half), in_specs=[anywhere] * 5, o...  110 us
    concatenate x1, other arithmetic, per_device(): return jnp.concatenate([top, low], axis=0)  3.11 us

profile of v2, /device:TPU:1, one launch (start us, length us, event | category | flops | bytes accessed | tf_op | source)
XLA Modules:
  0.0 113.3 jit_solution(6217522041162248152)
XLA Ops:
  0.0 110.2 %update.1 = (f32[256,1024]{1,0:T(8,128)}, f32[256,1024]{1,0:T(8,128)}) custom-call(f32[512,1024]{1,0:T(8,128)} %tr.1, f32[32,512]{1,0:T(8,128)} %bitcast.6, f32[32,256]{1,0:T(8,128)} %bitcast.7, f32[6,32,256]{2,1,0:T(8,128)} %bitcast.4, f32[6,32,256]{2,1,0:T(8,128)} %bitcast.5), custom_call_target="tpu_custom_call" | custom-call | tf_op jit(solution)/shard_map/update/pallas_call | solution.py:465
  110.2 3.1 %pad_maximum_fusion = f32[512,1024]{1,0:T(8,128)} fusion(f32[256,1024]{1,0:T(8,128)} %get-tuple-element.8, f32[256,1024]{1,0:T(8,128)} %get-tuple-element.7), kind=kLoop, calls=%fused_computation | loop fusion | flops 524288 | bytes 4194304 | tf_op jit(solution)/shard_map/concatenate | solution.py:502

commit v3 on v2

--- a/solution.py
+++ b/solution.py
@@ -33,12 +33,6 @@
 
 
 def mul(stacked, x):
-    hi, lo = split(x)
-    both = dot(stacked[...], hi)
-    return both[:B] + (both[B:] + dot(stacked[:B], lo))
-
-
-def narrow(stacked, x):
     both = dot(stacked[...], jnp.concatenate(split(x), axis=1))
     return both[:B, :W] + (both[:B, W:] + both[B:, :W])
 
@@ -57,10 +51,10 @@
 
 
 def kernel(
-    tr, vh, th, nr, nf, top_out, low_out,
-    WS, LB, PB, A4, SND, SC, OB, X0, X1, X2,
+    tr, vh, th, nr, nf, out,
+    WS, LB, PB, A4, SND, SC, X0, X1, X2,
     VT, VN, TT, FT, YT, YN,
-    ld, lda, ring_s, ring_r, pg_s, pg_r, sib_s, sib_r, late_s, late_r, top_s, top_r, st,
+    ld, lda, ring_s, ring_r, pg_s, pg_r, sib_s, sib_r, late_s, late_r, top_s, top_r,
 ):
     r = lax.axis_index("row")
     y = lax.axis_index("col")
@@ -96,7 +90,7 @@
             pltpu.make_async_copy(nr.at[s], WS.at[s], ld.at[1]).start()
 
     for c in range(4):
-        pltpu.make_async_copy(tr.at[:, c * B : (c + 1) * B], A4.at[c], lda.at[c]).start()
+        pltpu.make_async_copy(tr.at[:, c * B : (c + 1) * B], A4.at[c], lda).start()
 
     barrier = pltpu.get_barrier_semaphore()
 
@@ -228,16 +222,16 @@
     own2 = pltpu.make_async_copy(WS.at[4:6], PB.at[2, :, d2, mine, :], pg_r.at[2])
     own2.start()
 
-    for t in range(2):
-        for q in range(3):
-            ring_step(q, t)
+    for q in range(3):
+        ring_step(q, 0)
     arrived(PB.at[0, core, :, mine, :], pg_r.at[0])
+    ring_begin(3)
+    for q in range(3):
+        ring_step(q, 1)
+    ring_begin(4)
     for q in range(3):
         ring_step(q, 2)
-    ring_begin(3)
-    ring_begin(4)
-    own2.wait()
-    ring_begin(5)
+    ring_step(3, 0)
     for n in range(2):
         ring_step(n, 3)
         flat = LB[n]
@@ -245,6 +239,8 @@
         put(VN.at[n], jnp.transpose(flat))
     ring_step(2, 3)
     put(TT, triangle(LB[2]))
+    ring_step(4, 0)
+    own2.wait()
 
     def spread(k):
         other = 2 - 2 * z0
@@ -259,55 +255,42 @@
             device_id=(row(to, d1, d2), y), device_id_type=MESH,
         )
 
-    def leaf(pair, _):
-        quarters = [spread(2 * pair), spread(2 * pair + 1)]
-        for quarter in quarters:
-            pltpu.make_async_copy(tr.at[:, 0:B], A4.at[quarter], lda.at[quarter]).wait()
-        scaled = []
-        for quarter in quarters:
-            inner = mul(VT.at[0], A4[quarter, :B, :]) + mul(VT.at[1], A4[quarter, B:, :])
-            scaled.append(mul(TT, inner))
-        for quarter, value in zip(quarters, scaled):
-            SC[quarter] = value
-            leafed = A4[quarter, :B, :] - mul(VN.at[0], value)
-            SND[quarter, 0] = leafed[:, :W]
-            SND[quarter, 1] = leafed[:, W:]
-        for h in range(2):
-            a_copy(h, 2 * pair).start()
-
-            @pl.when(pair == 0)
-            def _():
-                a_copy(h, 2 * pair + 1).start()
-
-            @pl.when(pair == 1)
-            def _():
+    def leaf(h):
+        cols = slice(h * W, (h + 1) * W)
+        quarters = [spread(k) for k in range(4)]
+        if h == 0:
+            arrived(A4, lda)
+        inner = [mul(VT.at[0], A4[q, :B, cols]) + mul(VT.at[1], A4[q, B:, cols]) for q in quarters]
+        scaled = [mul(TT, v) for v in inner]
+        taken = [mul(VN.at[0], v) for v in scaled]
+        for k, q in enumerate(quarters):
+            SND[q, h] = A4[q, :B, cols] - taken[k]
+            if k < 3:
+                a_copy(h, k).start()
+            else:
                 pltpu.make_async_copy(SND.at[d0, h], X0.at[h, d0], top_r.at[0, h]).start()
-
-        return 0
-
-    def remainder(quarter, _):
-        OB[quarter] = A4[quarter, B:, :] - mul(VN.at[1], SC[quarter])
-        pltpu.make_async_copy(
-            OB.at[quarter], low_out.at[:, pl.ds(pl.multiple_of(quarter * B, B), B)], st
-        ).start()
-        return 0
-
-    lax.fori_loop(0, 1, leaf, 0)
-    ring_step(3, 0)
-    ring_step(4, 0)
-    lax.fori_loop(1, 2, leaf, 0)
+        for k, q in enumerate(quarters):
+            SC[q, h] = scaled[k]
+
+    def remainder(h):
+        cols = slice(h * W, (h + 1) * W)
+        taken = [mul(VN.at[1], SC[c, h]) for c in range(4)]
+        for c in range(4):
+            out[B:, c * B + h * W : c * B + (h + 1) * W] = A4[c, B:, cols] - taken[c]
+
+    leaf(0)
     ring_step(3, 1)
+    leaf(1)
     ring_step(4, 1)
-    ring_step(5, 0)
-    lax.fori_loop(0, 1, remainder, 0)
+    ring_begin(5)
     ring_step(3, 2)
+    remainder(0)
     ring_step(4, 2)
-    ring_step(5, 1)
     arrived(PB.at[1, core, :, mine, :], pg_r.at[1])
     ring_begin(6)
     ring_step(3, 3)
     ring_step(4, 3)
-    ring_step(5, 2)
+    ring_step(5, 0)
     ring_begin(7)
 
     def sibling_wait(phase):
@@ -315,33 +298,27 @@
             arrived(PB.at[phase, 1 - core, 2 * part : 2 * part + 2], sib_r.at[SHARED[2 * phase + part]])
 
     def prepare(q):
-        def body(e, _):
-            level, n = div(e, 2), rem(e, 2)
+        for e in range(4):
+            level, n = e // 2, e % 2
             k = (2 - level) * n
             p = k + 1 + level
             put(FT.at[e], triangle(PB[q, level, k]))
             turned = PB[q, level, p]
             put(YT.at[e], turned)
             put(YN.at[e], jnp.transpose(turned))
-            return 0
-
-        lax.fori_loop(0, 4, body, 0)
 
     def apply(X, h):
-        def body(level, _):
+        tops = [X[h, i] for i in range(4)]
+        for level in range(2):
             at = [((2 - level) * n, (2 - level) * n + 1 + level) for n in range(2)]
-            for n in range(2):
-                k, p = at[n]
-                e = 2 * level + n
-                lead = X[h, k]
-                follow = X[h, p]
-                summed = lead + narrow(YT.at[e], follow)
-                coupling = narrow(FT.at[e], summed)
-                X[h, k] = lead - coupling
-                X[h, p] = follow - narrow(YN.at[e], coupling)
-            return 0
-
-        lax.fori_loop(0, 2, body, 0)
+            summed = [tops[k] + mul(YT.at[2 * level + n], tops[p]) for n, (k, p) in enumerate(at)]
+            coupling = [mul(FT.at[2 * level + n], v) for n, v in enumerate(summed)]
+            taken = [mul(YN.at[2 * level + n], v) for n, v in enumerate(coupling)]
+            for n, (k, p) in enumerate(at):
+                tops[k] = tops[k] - coupling[n]
+                tops[p] = tops[p] - taken[n]
+        for i in range(4):
+            X[h, i] = tops[i]
 
     kept_b = z2 + 2 * z0
 
@@ -361,7 +338,7 @@
 
     def home(h):
         quarter = rem(d2 - d1 + 4, 4)
-        return top_out.at[:, pl.ds(pl.multiple_of(quarter * B + h * W, W), W)]
+        return out.at[:B, pl.ds(pl.multiple_of(quarter * B + h * W, W), W)]
 
     def f_copy(h, t):
         i = rem(d2 + t, 4)
@@ -398,14 +375,16 @@
         apply(X0, h)
         send(b_copy, h, self_b, lambda: pltpu.make_async_copy(X0.at[h, kept_b], X1.at[h, d1], top_r.at[1, h]))
         if h == 0:
-            ring_step(5, 3)
-            for t in (2, 1, 3):
-                late(t).start()
+            ring_step(5, 1)
             ring_step(6, 0)
-            ring_step(7, 0)
+    ring_step(5, 2)
+    ring_step(7, 0)
+    ring_step(5, 3)
+    for t in (2, 1, 3):
+        late(t).start()
     ring_step(6, 1)
     ring_step(7, 1)
-    lax.fori_loop(1, 4, remainder, 0)
+    remainder(1)
     ring_step(6, 2)
     ring_step(7, 2)
     ring_step(6, 3)
@@ -428,7 +407,7 @@
         send(f_copy, h, None, lambda: pltpu.make_async_copy(X2.at[h, d2], home(h), top_r.at[3, h]))
 
     for h in range(2):
-        arrived(top_out.at[:, 0 : 4 * W], top_r.at[3, h])
+        arrived(out.at[:B, 0 : 4 * W], top_r.at[3, h])
 
     for q in range(8):
         rows = pl.ds(0, 7 * S)
@@ -453,40 +432,35 @@
         def _():
             arrived(all_, sem)
 
-    arrived(OB, st)
-
 
 def per_device(trailing, reflectors, leaf_factor, node_reflect, node_factor):
     anywhere = pl.BlockSpec(memory_space=pl.ANY)
     dma = pltpu.SemaphoreType.DMA
     tops = pltpu.VMEM((2, 4, B, W), F32)
     nodes = pltpu.VMEM((4, 2 * B, B), BF16)
-    half = jax.ShapeDtypeStruct((B, trailing.shape[1]), F32)
-    top, low = pl.pallas_call(
+    return pl.pallas_call(
         kernel,
-        out_shape=(half, half),
+        out_shape=pltpu.VMEM(trailing.shape, F32),
         in_specs=[anywhere] * 5,
-        out_specs=(anywhere, anywhere),
+        out_specs=pl.BlockSpec(memory_space=pltpu.VMEM),
         scratch_shapes=[
             pltpu.VMEM((6, S, B), F32),
             pltpu.VMEM((3, B, B), F32),
             pltpu.VMEM((3, 2, 4, B, B), F32),
             pltpu.VMEM((4, 2 * B, B), F32),
             pltpu.VMEM((4, 2, B, W), F32),
-            pltpu.VMEM((4, B, B), F32),
-            pltpu.VMEM((4, B, B), F32),
+            pltpu.VMEM((4, 2, B, W), F32),
             tops, tops, tops,
             pltpu.VMEM((2, 2 * B, B), BF16),
             pltpu.VMEM((2, 2 * B, B), BF16),
             pltpu.VMEM((2 * B, B), BF16),
             nodes, nodes, nodes,
-            dma((2,)), dma((4,)),
+            dma((2,)), dma,
             dma((8,)), dma((8, 2, 4)),
             dma((2,)), dma((3,)),
             dma((8,)), dma((8,)),
             dma, dma,
             dma((4,)), dma((4, 2)),
-            dma,
         ],
         compiler_params=pltpu.CompilerParams(
             collective_id=0, has_side_effects=True, vmem_limit_bytes=56 * 1024 * 1024
@@ -499,7 +473,6 @@
         jnp.swapaxes(node_reflect, 1, 2),
         jnp.swapaxes(node_factor, 1, 2),
     )
-    return jnp.concatenate([top, low], axis=0)
 
 
 def solution(mesh):

time: 114 us -> 105 us (0.921)
  Pallas kernels: 110 us -> 104 us
  other arithmetic: 3.11 us -> 0 us
  local copies, waits for them, and re-layouts: 0 us -> 1.32 us
    pallas_call x1, Pallas kernels: 110 us -> 104 us  [per_device(): pl.pallas_call(kernel, out_shape=pltpu.VMEM(trailing.shape, F32), in_spec...]
    concatenate x1 -> x0, other arithmetic: 3.11 us -> none  [per_device(): return jnp.concatenate([top, low], axis=0)]
    unnamed x0 -> x1, local copies, waits for them, and re-layouts: none -> 1.32 us
where the time goes in v3:
time: 105 us
  Pallas kernels  104 us (99%)
  local copies, waits for them, and re-layouts  1.32 us (1%)
    pallas_call x1, Pallas kernels, per_device(): pl.pallas_call(kernel, out_shape=pltpu.VMEM(trailing.shape, F32), in_spec...  104 us

profile of v3, /device:TPU:1, one launch (start us, length us, event | category | flops | bytes accessed | tf_op | source)
XLA Modules:
  0.0 105.2 jit_solution(3912517525743041228)
XLA Ops:
  0.0 103.8 %update.1 = f32[512,1024]{1,0:T(8,128)S(1)} custom-call(f32[512,1024]{1,0:T(8,128)} %tr.1, f32[32,512]{1,0:T(8,128)} %bitcast.6, f32[32,256]{1,0:T(8,128)} %bitcast.7, f32[6,32,256]{2,1,0:T(8,128)} %bitcast.4, f32[6,32,256]{2,1,0:T(8,128)} %bitcast.5), custom_call_target="tpu_custom_call" | custom-call | tf_op jit(solution)/shard_map/update/pallas_call | solution.py:441
  103.9 1.3 %copy.7 = f32[512,1024]{1,0:T(8,128)} copy(f32[512,1024]{1,0:T(8,128)S(1)} %update.1) | data formatting | bytes 4194304

commit v4 on v3

--- a/solution.py
+++ b/solution.py
@@ -8,7 +8,7 @@
 B = 256
 S = 32
 W = 128
-SHARED = (3, 4, 6, 7)
+SHARED = (3, 4, 6, 7, 5)
 MESH = pl.DeviceIdType.MESH
 F32 = jnp.float32
 BF16 = jnp.bfloat16
@@ -54,7 +54,7 @@
     tr, vh, th, nr, nf, out,
     WS, LB, PB, A4, SND, SC, X0, X1, X2,
     VT, VN, TT, FT, YT, YN,
-    ld, lda, ring_s, ring_r, pg_s, pg_r, sib_s, sib_r, late_s, late_r, top_s, top_r,
+    ld, lda, ring_s, ring_r, pg_s, pg_r, sib_s, sib_r, top_s, top_r,
 ):
     r = lax.axis_index("row")
     y = lax.axis_index("col")
@@ -65,6 +65,11 @@
     z0 = div(d0, 2)
     z1 = rem(d1, 2)
     z2 = div(d1, 2)
+    x0 = rem(d2, 2)
+    x1 = div(d2, 2)
+    group = rem(x0 + z1, 2)
+    flip = rem(x1 + z2, 2)
+    turn = rem(core + z1, 2)
 
     def row(a, b, c):
         return a + 4 * b + 16 * c
@@ -101,16 +106,19 @@
     greet(r, left)
     for t in range(1, 4):
         greet(row(rem(d0 + t, 4), d1, d2), y)
-        greet(row(d0, d1, rem(d2 + t, 4)), y)
-    held = rem(d2 - d1 + 4, 4)
     self_a = z2 == core
     self_b = z1 == z0
-    self_c = jnp.logical_and(self_a, held == core + 2 * z1)
+    self_c = d2 == 3 * rem(z1 + z2, 2)
+    self_d = group == core
     for t in range(4):
+        back_d0 = rem(core + t, 2) + 2 * z0
+        back_d2 = turn + 2 * rem(x1 + t // 2, 2)
         sources = (
             (self_a, row(z2 + 2 * z0, rem(d1 + t, 4), d2)),
             (self_b, row(core + 2 * z1, rem(d1 + t, 4), d2)),
-            (self_c, row(rem(held, 2) + 2 * z0, div(held, 2) + 2 * core, rem(d2 + t, 4))),
+            (self_c, row(d0, flip + 2 * group, rem(d2 + t, 4))),
+            (self_d, row(group + 2 * z0, d1, rem(d2 + t, 4))),
+            (self_d, row(back_d0, d1, back_d2)),
         )
         for own, source in sources:
             if t:
@@ -125,8 +133,8 @@
         pltpu.make_async_copy(ref, ref, sem).wait()
 
     arrived(LB.at[:, mine, :], ld.at[0])
-    expected = 8 + 9
-    for own in (self_a, self_b, self_c):
+    expected = 5 + 15
+    for own in (self_a, self_b, self_c, self_d, self_d):
         expected = expected + jnp.where(own, 0, 1)
     pl.semaphore_wait(barrier, expected)
 
@@ -138,7 +146,7 @@
         if q < 5:
             return PB.at[0, core, 2 * (q - 3) : 2 * (q - 2), rows, :]
         if q == 5:
-            return PB.at[2, :, d2, rows, :]
+            return PB.at[2, core, :, rows, :]
         return PB.at[1, core, 2 * (q - 6) : 2 * (q - 5), rows, :]
 
     def ring(q, way, t):
@@ -219,19 +227,38 @@
             def _():
                 pltpu.make_async_copy(WS.at[2 + level], PB.at[1, level, d1, mine, :], pg_r.at[1]).start()
 
-    own2 = pltpu.make_async_copy(WS.at[4:6], PB.at[2, :, d2, mine, :], pg_r.at[2])
-    own2.start()
+    def pre2(level, side):
+        return pltpu.make_async_remote_copy(
+            WS.at[4 + level], PB.at[2, level, d2, mine, :], pg_s.at[2], pg_r.at[2],
+            device_id=(row(level + 2 * z0, d1, turn + 2 * side), y), device_id_type=MESH,
+        )
+
+    def pre2_own(level, side):
+        return jnp.logical_and(self_d, jnp.logical_and(core == level, x1 == side))
+
+    for level in range(2):
+        for side in range(2):
+
+            @pl.when(jnp.logical_not(pre2_own(level, side)))
+            def _():
+                pre2(level, side).start()
+
+            @pl.when(pre2_own(level, side))
+            def _():
+                pltpu.make_async_copy(WS.at[4 + level], PB.at[2, level, d2, mine, :], pg_r.at[2]).start()
 
     for q in range(3):
         ring_step(q, 0)
     arrived(PB.at[0, core, :, mine, :], pg_r.at[0])
     ring_begin(3)
+    ring_begin(4)
     for q in range(3):
         ring_step(q, 1)
-    ring_begin(4)
+    ring_step(3, 0)
+    ring_step(4, 0)
     for q in range(3):
         ring_step(q, 2)
-    ring_step(3, 0)
+    ring_step(3, 1)
     for n in range(2):
         ring_step(n, 3)
         flat = LB[n]
@@ -239,8 +266,7 @@
         put(VN.at[n], jnp.transpose(flat))
     ring_step(2, 3)
     put(TT, triangle(LB[2]))
-    ring_step(4, 0)
-    own2.wait()
+    ring_step(4, 1)
 
     def spread(k):
         other = 2 - 2 * z0
@@ -279,23 +305,22 @@
             out[B:, c * B + h * W : c * B + (h + 1) * W] = A4[c, B:, cols] - taken[c]
 
     leaf(0)
-    ring_step(3, 1)
+    ring_step(3, 2)
     leaf(1)
-    ring_step(4, 1)
-    ring_begin(5)
-    ring_step(3, 2)
-    remainder(0)
     ring_step(4, 2)
     arrived(PB.at[1, core, :, mine, :], pg_r.at[1])
     ring_begin(6)
     ring_step(3, 3)
     ring_step(4, 3)
-    ring_step(5, 0)
     ring_begin(7)
+    ring_step(6, 0)
 
     def sibling_wait(phase):
-        for part in range(2):
-            arrived(PB.at[phase, 1 - core, 2 * part : 2 * part + 2], sib_r.at[SHARED[2 * phase + part]])
+        if phase == 2:
+            arrived(PB.at[2, 1 - core], sib_r.at[5])
+        else:
+            for part in range(2):
+                arrived(PB.at[phase, 1 - core, 2 * part : 2 * part + 2], sib_r.at[SHARED[2 * phase + part]])
 
     def prepare(q):
         for e in range(4):
@@ -304,15 +329,28 @@
             p = k + 1 + level
             put(FT.at[e], triangle(PB[q, level, k]))
             turned = PB[q, level, p]
-            put(YT.at[e], turned)
             put(YN.at[e], jnp.transpose(turned))
+            if q == 0:
+                put(YT.at[e], turned)
+            else:
+                for c in range(2):
+                    cols = slice(c * W, (c + 1) * W)
+                    hi, lo = split(mul(FT.at[e], turned[:, cols]))
+                    YT[e, :B, cols] = hi
+                    YT[e, B:, cols] = lo
 
     def apply(X, h):
         tops = [X[h, i] for i in range(4)]
         for level in range(2):
             at = [((2 - level) * n, (2 - level) * n + 1 + level) for n in range(2)]
-            summed = [tops[k] + mul(YT.at[2 * level + n], tops[p]) for n, (k, p) in enumerate(at)]
-            coupling = [mul(FT.at[2 * level + n], v) for n, v in enumerate(summed)]
+            if X is X0:
+                summed = [tops[k] + mul(YT.at[2 * level + n], tops[p]) for n, (k, p) in enumerate(at)]
+                coupling = [mul(FT.at[2 * level + n], v) for n, v in enumerate(summed)]
+            else:
+                coupling = [
+                    mul(FT.at[2 * level + n], tops[k]) + mul(YT.at[2 * level + n], tops[p])
+                    for n, (k, p) in enumerate(at)
+                ]
             taken = [mul(YN.at[2 * level + n], v) for n, v in enumerate(coupling)]
             for n, (k, p) in enumerate(at):
                 tops[k] = tops[k] - coupling[n]
@@ -333,40 +371,31 @@
         i = rem(d1 + t, 4)
         return pltpu.make_async_remote_copy(
             X1.at[h, i], X2.at[h, d2], top_s.at[2], top_r.at[2, h],
-            device_id=(row(z2 + 2 * z0, i, rem(core + 2 * z1 + i, 4)), y), device_id_type=MESH,
+            device_id=(row(d0, i, rem(z2 + i, 2) + 2 * rem(z1 + div(i, 2), 2)), y), device_id_type=MESH,
         )
 
     def home(h):
-        quarter = rem(d2 - d1 + 4, 4)
+        quarter = core + 2 * flip
         return out.at[:B, pl.ds(pl.multiple_of(quarter * B + h * W, W), W)]
 
     def f_copy(h, t):
         i = rem(d2 + t, 4)
         return pltpu.make_async_remote_copy(
             X2.at[h, i], home(h), top_s.at[3], top_r.at[3, h],
-            device_id=(row(d0, d1, i), y), device_id_type=MESH,
+            device_id=(row(group + 2 * z0, d1, i), y), device_id_type=MESH,
         )
 
     def send(copy, h, own, local):
         for t in (2, 1, 3):
             copy(h, t).start()
-        if own is None:
+
+        @pl.when(jnp.logical_not(own))
+        def _():
+            copy(h, 0).start()
+
+        @pl.when(own)
+        def _():
             local().start()
-        else:
-
-            @pl.when(jnp.logical_not(own))
-            def _():
-                copy(h, 0).start()
-
-            @pl.when(own)
-            def _():
-                local().start()
-
-    def late(t):
-        return pltpu.make_async_remote_copy(
-            PB.at[2, :, d2], PB.at[2, :, d2], late_s, late_r,
-            device_id=(row(d0, d1, rem(d2 + t, 4)), y), device_id_type=MESH,
-        )
 
     sibling_wait(0)
     prepare(0)
@@ -375,53 +404,54 @@
         apply(X0, h)
         send(b_copy, h, self_b, lambda: pltpu.make_async_copy(X0.at[h, kept_b], X1.at[h, d1], top_r.at[1, h]))
         if h == 0:
-            ring_step(5, 1)
-            ring_step(6, 0)
-    ring_step(5, 2)
-    ring_step(7, 0)
-    ring_step(5, 3)
-    for t in (2, 1, 3):
-        late(t).start()
+            ring_step(7, 0)
     ring_step(6, 1)
     ring_step(7, 1)
-    remainder(1)
+    arrived(PB.at[2, core, :, mine, :], pg_r.at[2])
     ring_step(6, 2)
     ring_step(7, 2)
+    ring_begin(5)
     ring_step(6, 3)
+    remainder(0)
     ring_step(7, 3)
+    ring_step(5, 0)
     sibling_wait(1)
     prepare(1)
 
 
+    ring_step(5, 1)
     for h in range(2):
         arrived(X1.at[h], top_r.at[1, h])
         apply(X1, h)
         send(c_copy, h, self_c, lambda: pltpu.make_async_copy(X1.at[h, d1], X2.at[h, d2], top_r.at[2, h]))
-
-    arrived(PB.at[2, :, 0:3], late_r)
+        if h == 0:
+            for t in range(2, 4):
+                ring_step(5, t)
+            remainder(1)
+    sibling_wait(2)
     prepare(2)
 
     for h in range(2):
         arrived(X2.at[h], top_r.at[2, h])
         apply(X2, h)
-        send(f_copy, h, None, lambda: pltpu.make_async_copy(X2.at[h, d2], home(h), top_r.at[3, h]))
+        send(f_copy, h, self_d, lambda: pltpu.make_async_copy(X2.at[h, d2], home(h), top_r.at[3, h]))
 
     for h in range(2):
         arrived(out.at[:B, 0 : 4 * W], top_r.at[3, h])
 
     for q in range(8):
         rows = pl.ds(0, 7 * S)
-        arrived(LB.at[q, rows] if q < 3 else PB.at[0, 0, 0:2, rows], ring_s.at[q])
+        arrived(LB.at[q, rows] if q < 3 else PB.at[0, 0, 0 : 4 if q == 5 else 2, rows], ring_s.at[q])
     for q in SHARED:
-        arrived(PB.at[0, 0, 0:2], sib_s.at[q])
+        arrived(PB.at[0, 0, 0 : 4 if q == 5 else 2], sib_s.at[q])
     arrived(WS.at[0:3], pg_s.at[0])
-    arrived(PB.at[2, :, 0:3], late_s)
     arrived(X0.at[:, 0:3], top_s.at[0])
-    arrived(X0.at[:, 0:3], top_s.at[3])
     for own, sem, few, all_ in (
         (self_a, pg_s.at[1], WS.at[0:3], WS.at[0:4]),
         (self_b, top_s.at[1], X0.at[:, 0:3], X0),
         (self_c, top_s.at[2], X1.at[:, 0:3], X1),
+        (self_d, pg_s.at[2], WS.at[0:3], WS.at[0:4]),
+        (self_d, top_s.at[3], X2.at[:, 0:3], X2),
     ):
 
         @pl.when(own)
@@ -457,9 +487,8 @@
             nodes, nodes, nodes,
             dma((2,)), dma,
             dma((8,)), dma((8, 2, 4)),
-            dma((2,)), dma((3,)),
+            dma((3,)), dma((3,)),
             dma((8,)), dma((8,)),
-            dma, dma,
             dma((4,)), dma((4, 2)),
         ],
         compiler_params=pltpu.CompilerParams(

time: 105 us -> 104 us (level)
  the two profiles are of different devices: /device:TPU:1 before, /device:TPU:192 now
where the time goes in v4:
time: 104 us
  Pallas kernels  103 us (99%)
  local copies, waits for them, and re-layouts  1.32 us (1%)
    pallas_call x1, Pallas kernels, per_device(): pl.pallas_call(kernel, out_shape=pltpu.VMEM(trailing.shape, F32), in_spec...  103 us

profile of v4, /device:TPU:192, one launch (start us, length us, event | category | flops | bytes accessed | tf_op | source)
XLA Modules:
  0.0 104.1 jit_solution(15421862375070566274)
XLA Ops:
  0.0 102.8 %update.1 = f32[512,1024]{1,0:T(8,128)S(1)} custom-call(f32[512,1024]{1,0:T(8,128)} %tr.1, f32[32,512]{1,0:T(8,128)} %bitcast.6, f32[32,256]{1,0:T(8,128)} %bitcast.7, f32[6,32,256]{2,1,0:T(8,128)} %bitcast.4, f32[6,32,256]{2,1,0:T(8,128)} %bitcast.5), custom_call_target="tpu_custom_call" | custom-call | tf_op jit(solution)/shard_map/update/pallas_call | solution.py:471
  102.8 1.3 %copy.7 = f32[512,1024]{1,0:T(8,128)} copy(f32[512,1024]{1,0:T(8,128)S(1)} %update.1) | data formatting | bytes 4194304

commit v5 on v4

--- a/solution.py
+++ b/solution.py
@@ -322,6 +322,15 @@
             for part in range(2):
                 arrived(PB.at[phase, 1 - core, 2 * part : 2 * part + 2], sib_r.at[SHARED[2 * phase + part]])
 
+    def prepare_first(level):
+        for n in range(2):
+            k = (2 - level) * n
+            e = 2 * level + n
+            turned = PB[0, level, k + 1 + level]
+            put(FT.at[e], triangle(PB[0, level, k]))
+            put(YT.at[e], turned)
+            put(YN.at[e], jnp.transpose(turned))
+
     def prepare(q):
         for e in range(4):
             level, n = e // 2, e % 2
@@ -330,14 +339,11 @@
             put(FT.at[e], triangle(PB[q, level, k]))
             turned = PB[q, level, p]
             put(YN.at[e], jnp.transpose(turned))
-            if q == 0:
-                put(YT.at[e], turned)
-            else:
-                for c in range(2):
-                    cols = slice(c * W, (c + 1) * W)
-                    hi, lo = split(mul(FT.at[e], turned[:, cols]))
-                    YT[e, :B, cols] = hi
-                    YT[e, B:, cols] = lo
+            for c in range(2):
+                cols = slice(c * W, (c + 1) * W)
+                hi, lo = split(mul(FT.at[e], turned[:, cols]))
+                YT[e, :B, cols] = hi
+                YT[e, B:, cols] = lo
 
     def apply(X, h):
         tops = [X[h, i] for i in range(4)]
@@ -386,7 +392,7 @@
         )
 
     def send(copy, h, own, local):
-        for t in (2, 1, 3):
+        for t in (1, 3, 2) if copy is b_copy else (2, 1, 3):
             copy(h, t).start()
 
         @pl.when(jnp.logical_not(own))
@@ -397,8 +403,9 @@
         def _():
             local().start()
 
+    prepare_first(core)
     sibling_wait(0)
-    prepare(0)
+    prepare_first(1 - core)
     for h in range(2):
         arrived(X0.at[h], top_r.at[0, h])
         apply(X0, h)

time: 104 us -> 104 us (level)
  the two profiles are of different devices: /device:TPU:192 before, /device:TPU:1 now
where the time goes in v5:
time: 104 us
  Pallas kernels  103 us (99%)
  local copies, waits for them, and re-layouts  1.32 us (1%)
    pallas_call x1, Pallas kernels, per_device(): pl.pallas_call(kernel, out_shape=pltpu.VMEM(trailing.shape, F32), in_spec...  103 us

profile of v5, /device:TPU:1, one launch (start us, length us, event | category | flops | bytes accessed | tf_op | source)
XLA Modules:
  0.0 104.1 jit_solution(2376391936722175027)
XLA Ops:
  0.0 102.7 %update.1 = f32[512,1024]{1,0:T(8,128)S(1)} custom-call(f32[512,1024]{1,0:T(8,128)} %tr.1, f32[32,512]{1,0:T(8,128)} %bitcast.6, f32[32,256]{1,0:T(8,128)} %bitcast.7, f32[6,32,256]{2,1,0:T(8,128)} %bitcast.4, f32[6,32,256]{2,1,0:T(8,128)} %bitcast.5), custom_call_target="tpu_custom_call" | custom-call | tf_op jit(solution)/shard_map/update/pallas_call | solution.py:478
  102.7 1.3 %copy.7 = f32[512,1024]{1,0:T(8,128)} copy(f32[512,1024]{1,0:T(8,128)S(1)} %update.1) | data formatting | bytes 4194304
